TPU v7x, 128 devices: a whole 4x4x4 slice. The times are simulated.
128 devices in a mesh: slab: 16 (over z, y), energy: 8 (over x, core).
Axes of the slice: x: 4, y: 4, z: 4, core: 2. Of those that a mesh axis runs over, the one named last changes fastest.
Arguments:
- source: float32 [32, 2, 16, 192, 128], P('slab', None, 'energy'), may hold values from -1.2 to 1.2
- onsite_block: float32 [192, 192], replicated, may hold values from -1.3 to 1.3, as said below
- hopping_block: float32 [192, 192], replicated, may hold values from -0.5 to 1.5
- potential_table: float32 [16, 192], replicated, may hold values from -0.5 to 0.5
- slab_profile: int32 [32], P('slab'), may hold values from 0 to 15
- occupation: float32 [32, 16, 192], P('slab', 'energy'), may hold values from 0.1 to 1
- coupling: float32 [4], replicated, may hold values from 0.02 to 0.08
- phonon_shift: int32 [4], replicated, may hold values from 1 to 2, as said below
Outputs:
- amplitude: float32 [32, 2, 16, 192, 128], P('slab', None, 'energy')
- density: float32 [32, 16, 192], P('slab', 'energy')
Inputs may be any that keep to these rules, and one draw needn't show every extreme that they name: `phonon_shift`: some mode shifts by exactly 2 points and some by exactly 1. `onsite_block`: symmetric.
All inputs are finite; a program needn't handle non-finite values.
Results may differ from a plain program's by a relative error of at most 0.0003.
Values sent between devices are 32-bit elements; how exact they have to be, the bound alone decides.
No kernel may reach another device: no remote copies, remote signals or barrier semaphores. Data moves between devices by JAX's collectives and lax.ppermute only.
A program may use at most 128 MiB of HBM per device.

v0:
```python
import jax
import jax.numpy as jnp
from jax import lax
from jax.sharding import PartitionSpec as P

broadening = 0.05
energy_low = -1.2
energy_step = 0.15


def padded(block, sides, width):
    for axis, dim in sides:
        count = lax.axis_size(axis)
        forward = [(i, i + 1) for i in range(count - 1)]
        backward = [(target, source) for source, target in forward]
        low = lax.ppermute(
            lax.slice_in_dim(block, block.shape[dim] - width, None, axis=dim), axis, forward
        )
        high = lax.ppermute(lax.slice_in_dim(block, 0, width, axis=dim), axis, backward)
        block = jnp.concatenate([low, block, high], axis=dim)
    return block


def shifted(array, axis, by):
    count = lax.axis_size(axis)
    pairs = [(i, i + by) for i in range(count) if 0 <= i + by < count]
    return lax.ppermute(array, axis, pairs)


def matmul_exact(left, right):
    return jnp.matmul(left, right, precision=lax.Precision.HIGHEST)


def complex_product(left, right):
    real = matmul_exact(left[..., 0, :, :, :], right[..., 0, :, :, :]) - matmul_exact(
        left[..., 1, :, :, :], right[..., 1, :, :, :]
    )
    imag = matmul_exact(left[..., 0, :, :, :], right[..., 1, :, :, :]) + matmul_exact(
        left[..., 1, :, :, :], right[..., 0, :, :, :]
    )
    return jnp.stack([real, imag], axis=-4)


def invert(block):
    real = block[..., 0, :, :, :]
    imag = block[..., 1, :, :, :]
    real = 0.5 * (real + jnp.swapaxes(real, -1, -2))
    imag = 0.5 * (imag + jnp.swapaxes(imag, -1, -2))
    lower_imag = jnp.linalg.cholesky(imag)
    weighed = jax.scipy.linalg.cho_solve((lower_imag, True), real)
    schur = imag + matmul_exact(real, weighed)
    schur = 0.5 * (schur + jnp.swapaxes(schur, -1, -2))
    lower_schur = jnp.linalg.cholesky(schur)
    identity = jnp.broadcast_to(jnp.eye(schur.shape[-1], dtype=schur.dtype), schur.shape)
    schur_inverse = jax.scipy.linalg.cho_solve((lower_schur, True), identity)
    return jnp.stack([matmul_exact(weighed, schur_inverse), -schur_inverse], axis=-4)


def per_device(
    source,
    onsite_block,
    hopping_block,
    potential_table,
    slab_profile,
    occupation,
    coupling,
    phonon_shift,
):
    slab_count = occupation.shape[0]
    energy_count = occupation.shape[1]
    orbitals = onsite_block.shape[0]
    hop_t = hopping_block.T
    widened = padded(occupation, (("energy", 1),), energy_count)
    own_points = jnp.arange(energy_count, dtype=jnp.int32)[:, None]
    all_points = jnp.arange(3 * energy_count, dtype=jnp.int32)[None, :]
    weights = jnp.zeros((energy_count, 3 * energy_count), jnp.float32)
    for mode in range(phonon_shift.shape[0]):
        above = (all_points == own_points + energy_count + phonon_shift[mode]).astype(jnp.float32)
        below = (all_points == own_points + energy_count - phonon_shift[mode]).astype(jnp.float32)
        weights = weights + coupling[mode] * (above + below)
    damping = jnp.einsum("ek,skb->seb", weights, widened, precision=lax.Precision.HIGHEST)
    chosen = (
        slab_profile[:, None] == jnp.arange(potential_table.shape[0], dtype=jnp.int32)[None, :]
    ).astype(jnp.float32)
    potential = matmul_exact(chosen, potential_table)
    first_point = lax.axis_index("energy") * energy_count
    energies = energy_low + energy_step * (
        first_point + jnp.arange(energy_count, dtype=jnp.int32)
    ).astype(jnp.float32)
    identity = jnp.eye(orbitals, dtype=jnp.float32)
    real_diag = (
        energies[None, :, None, None] * identity
        - onsite_block
        - potential[:, None, :, None] * identity
    )
    imag_diag = (broadening + damping)[..., None] * identity
    blocks = jnp.stack([real_diag, imag_diag], axis=1)
    inner = slab_count - 1
    position = jnp.arange(inner, dtype=jnp.int32)
    zeros_block = jnp.zeros((inner, energy_count, orbitals, orbitals), jnp.float32)
    first_real = (position == 0).astype(jnp.float32)[:, None, None, None] * identity + zeros_block
    last_real = (position == inner - 1).astype(jnp.float32)[
        :, None, None, None
    ] * identity + zeros_block
    first_part = jnp.stack([first_real, zeros_block], axis=1)
    last_part = jnp.stack([last_real, zeros_block], axis=1)
    right = jnp.concatenate([first_part, last_part, source[:inner]], axis=-1)

    def forward(carry, inputs):
        inverse, solved = carry
        block, rhs = inputs
        pivot = block - matmul_exact(hop_t, matmul_exact(inverse, hopping_block))
        rhs = rhs + matmul_exact(hop_t, solved)
        inverse = invert(pivot)
        solved = complex_product(inverse, rhs)
        return ((inverse, solved), (inverse, solved))

    start = (
        jnp.zeros((2, energy_count, orbitals, orbitals), jnp.float32),
        jnp.zeros(right.shape[1:], jnp.float32),
    )
    _, (inverses, solveds) = lax.scan(forward, start, (blocks[:inner], right))

    def backward(later, inputs):
        inverse, solved = inputs
        current = solved + complex_product(inverse, matmul_exact(hopping_block, later))
        return (current, current)

    _, eliminated = lax.scan(
        backward, jnp.zeros(right.shape[1:], jnp.float32), (inverses, solveds), reverse=True
    )
    from_first = eliminated[..., :orbitals]
    from_last = eliminated[..., orbitals : 2 * orbitals]
    interior = eliminated[..., 2 * orbitals :]
    own_block = blocks[inner] - matmul_exact(
        hop_t, matmul_exact(from_last[inner - 1], hopping_block)
    )
    lower = -matmul_exact(hop_t, matmul_exact(from_first[inner - 1], hop_t))
    own_right = source[inner] + matmul_exact(hop_t, interior[inner - 1])
    outgoing = jnp.concatenate(
        [
            -matmul_exact(hopping_block, matmul_exact(from_first[0], hop_t)),
            lower,
            matmul_exact(hopping_block, interior[0]),
        ],
        axis=-1,
    )
    incoming = shifted(outgoing, "slab", -1)
    pivot = own_block + incoming[..., :orbitals]
    upper = jnp.swapaxes(incoming[..., orbitals : 2 * orbitals], -1, -2)
    right_side = own_right + incoming[..., 2 * orbitals :]
    lower_now, upper_now, right_now, pivot_now = (lower, upper, right_side, pivot)
    for level in range((lax.axis_size("slab") - 1).bit_length()):
        distance = 1 << level
        scaled = complex_product(
            invert(pivot_now), jnp.concatenate([lower_now, upper_now, right_now], axis=-1)
        )
        from_below = shifted(scaled, "slab", distance)
        from_above = shifted(scaled, "slab", -distance)
        product_low = complex_product(lower_now, from_below)
        product_up = complex_product(upper_now, from_above)
        pivot_now = (
            pivot_now - product_low[..., orbitals : 2 * orbitals] - product_up[..., :orbitals]
        )
        right_now = right_now - product_low[..., 2 * orbitals :] - product_up[..., 2 * orbitals :]
        lower_now = -product_low[..., :orbitals]
        upper_now = -product_up[..., orbitals : 2 * orbitals]
    separator = complex_product(invert(pivot_now), right_now)
    previous = shifted(separator, "slab", 1)
    inner_solution = (
        interior
        + complex_product(from_first, matmul_exact(hop_t, previous))
        + complex_product(from_last, matmul_exact(hopping_block, separator))
    )
    amplitude = jnp.concatenate([inner_solution, separator[None]], axis=0)
    density = jnp.sum(amplitude[:, 0] ** 2 + amplitude[:, 1] ** 2, axis=-1)
    return (amplitude, density)


def solution(mesh):
    placed = (
        P("slab", None, "energy", None, None),
        P(),
        P(),
        P(),
        P("slab"),
        P("slab", "energy", None),
        P(),
        P(),
    )
    return jax.shard_map(
        per_device,
        mesh=mesh,
        in_specs=placed,
        out_specs=(P("slab", None, "energy", None, None), P("slab", "energy", None)),
        check_vma=False,
    )
```

profile of v0, /device:TPU:32, one launch (start us, length us, event | category | flops | bytes accessed | tf_op | source)
XLA Modules:
  0.0 1956.2 jit_solution(10982252885926560567)
XLA Ops:
  34.9 25.1 %custom-call.59 = f32[2,128,128]{2,1,0:T(8,128)} custom-call(f32[2,128,128]{2,1,0:T(8,128)} %copy.234), custom_call_target="Cholesky" | custom-call | tf_op jit(solution)/shard_map/while/body/eval_jaxpr/jit(cholesky)/cholesky | solution.py:49
  63.4 21.1 %custom-call.60 = f32[2,1,128,128]{2,3,1,0:T(8,128)} custom-call(f32[2,1,128,128]{3,2,1,0:T(8,128)} %get-tuple-element.193), custom_call_target="InvertDiagBlocksLowerTriangular" | custom-call | tf_op jit(solution)/shard_map/while/body/eval_jaxpr/jit(cholesky)/cholesky | solution.py:49
  106.6 41.1 %custom-call.62 = f32[2,2,128,128]{2,3,1,0:T(8,128)} custom-call(f32[2,2,128,128]{3,2,1,0:T(8,128)} %pad_maximum_fusion.57), custom_call_target="InvertDiagBlocksLowerTriangular" | custom-call | tf_op jit(solution)/shard_map/while/body/eval_jaxpr/jit(_cho_solve)/vmap()/triangular_solve | solution.py:50
  172.1 24.9 %custom-call.63 = f32[2,128,128]{2,1,0:T(8,128)} custom-call(f32[2,128,128]{2,1,0:T(8,128)} %copy.250), custom_call_target="Cholesky" | custom-call | tf_op jit(solution)/shard_map/while/body/eval_jaxpr/jit(cholesky)/cholesky | solution.py:53
  245.3 40.9 %custom-call.66 = f32[2,2,128,128]{2,3,1,0:T(8,128)} custom-call(f32[2,2,128,128]{3,2,1,0:T(8,128)} %pad_maximum_fusion.58), custom_call_target="InvertDiagBlocksLowerTriangular" | custom-call | tf_op jit(solution)/shard_map/while/body/eval_jaxpr/jit(_cho_solve)/vmap()/triangular_solve | solution.py:55
  322.5 32.6 %collective-permute-done.2 = f32[2,2,192,512]{3,2,1,0:T(8,128)S(1)} collective-permute-done((f32[2,2,192,512]{3,2,1,0:T(8,128)}, f32[2,2,192,512]{3,2,1,0:T(8,128)S(1)}, u32[]{:S(2)}, u32[]{:S(2)}) %collective-permute-start.2) | collective-permute-done | bytes 1572896 | tf_op jit(solution)/shard_map/ppermute | solution.py:27
  365.5 23.5 %custom-call.67 = f32[2,128,128]{2,1,0:T(8,128)S(1)} custom-call(f32[2,128,128]{2,1,0:T(8,128)S(1)} %copy.275), custom_call_target="Cholesky" | custom-call | tf_op jit(solution)/shard_map/jit(cholesky)/cholesky | solution.py:49
  391.9 21.1 %custom-call.68 = f32[2,1,128,128]{2,3,1,0:T(8,128)} custom-call(f32[2,1,128,128]{3,2,1,0:T(8,128)} %get-tuple-element.189), custom_call_target="InvertDiagBlocksLowerTriangular" | custom-call | tf_op jit(solution)/shard_map/jit(cholesky)/cholesky | solution.py:49
  434.1 40.9 %custom-call.70 = f32[2,2,128,128]{2,3,1,0:T(8,128)} custom-call(f32[2,2,128,128]{3,2,1,0:T(8,128)} %pad_maximum_fusion.59), custom_call_target="InvertDiagBlocksLowerTriangular" | custom-call | tf_op jit(solution)/shard_map/jit(_cho_solve)/vmap()/triangular_solve | solution.py:50
  492.2 23.5 %custom-call.71 = f32[2,128,128]{2,1,0:T(8,128)S(1)} custom-call(f32[2,128,128]{2,1,0:T(8,128)S(1)} %copy.291), custom_call_target="Cholesky" | custom-call | tf_op jit(solution)/shard_map/jit(cholesky)/cholesky | solution.py:53
  555.1 40.3 %custom-call.74 = f32[2,2,128,128]{2,3,1,0:T(8,128)S(1)} custom-call(f32[2,2,128,128]{3,2,1,0:T(8,128)} %pad_maximum_fusion.60), custom_call_target="InvertDiagBlocksLowerTriangular" | custom-call | tf_op jit(solution)/shard_map/jit(_cho_solve)/vmap()/triangular_solve | solution.py:55
  623.6 32.1 %collective-permute-done.4 = f32[2,2,192,512]{3,2,1,0:T(8,128)S(1)} collective-permute-done((f32[2,2,192,512]{3,2,1,0:T(8,128)S(1)}, f32[2,2,192,512]{3,2,1,0:T(8,128)S(1)}, u32[]{:S(2)}, u32[]{:S(2)}) %collective-permute-start.4) | collective-permute-done | bytes 1572896 | tf_op jit(solution)/shard_map/ppermute | solution.py:27
  686.8 25.1 %custom-call.75 = f32[2,128,128]{2,1,0:T(8,128)} custom-call(f32[2,128,128]{2,1,0:T(8,128)} %copy.321), custom_call_target="Cholesky" | custom-call | tf_op jit(solution)/shard_map/jit(cholesky)/cholesky | solution.py:49
  760.1 40.9 %custom-call.78 = f32[2,2,128,128]{2,3,1,0:T(8,128)} custom-call(f32[2,2,128,128]{3,2,1,0:T(8,128)} %pad_maximum_fusion.61), custom_call_target="InvertDiagBlocksLowerTriangular" | custom-call | tf_op jit(solution)/shard_map/jit(_cho_solve)/vmap()/triangular_solve | solution.py:50
  825.3 24.9 %custom-call.79 = f32[2,128,128]{2,1,0:T(8,128)} custom-call(f32[2,128,128]{2,1,0:T(8,128)} %copy.337), custom_call_target="Cholesky" | custom-call | tf_op jit(solution)/shard_map/jit(cholesky)/cholesky | solution.py:53
  898.5 41.1 %custom-call.82 = f32[2,2,128,128]{2,3,1,0:T(8,128)} custom-call(f32[2,2,128,128]{3,2,1,0:T(8,128)} %pad_maximum_fusion.62), custom_call_target="InvertDiagBlocksLowerTriangular" | custom-call | tf_op jit(solution)/shard_map/jit(_cho_solve)/vmap()/triangular_solve | solution.py:55
  965.5 33.1 %collective-permute-done.6 = f32[2,2,192,512]{3,2,1,0:T(8,128)S(1)} collective-permute-done((f32[2,2,192,512]{3,2,1,0:T(8,128)S(1)}, f32[2,2,192,512]{3,2,1,0:T(8,128)S(1)}, u32[]{:S(2)}, u32[]{:S(2)}) %collective-permute-start.6) | collective-permute-done | bytes 1572896 | tf_op jit(solution)/shard_map/ppermute | solution.py:27
  1000.3 27.5 %collective-permute-done.5 = f32[2,2,192,512]{3,2,1,0:T(8,128)S(1)} collective-permute-done((f32[2,2,192,512]{3,2,1,0:T(8,128)S(1)}, f32[2,2,192,512]{3,2,1,0:T(8,128)S(1)}, u32[]{:S(2)}, u32[]{:S(2)}) %collective-permute-start.5) | collective-permute-done | bytes 1572896 | tf_op jit(solution)/shard_map/ppermute | solution.py:27
  1051.3 25.1 %custom-call.83 = f32[2,128,128]{2,1,0:T(8,128)} custom-call(f32[2,128,128]{2,1,0:T(8,128)} %copy.353), custom_call_target="Cholesky" | custom-call | tf_op jit(solution)/shard_map/jit(cholesky)/cholesky | solution.py:49
  1124.8 41.1 %custom-call.86 = f32[2,2,128,128]{2,3,1,0:T(8,128)} custom-call(f32[2,2,128,128]{3,2,1,0:T(8,128)} %pad_maximum_fusion.63), custom_call_target="InvertDiagBlocksLowerTriangular" | custom-call | tf_op jit(solution)/shard_map/jit(_cho_solve)/vmap()/triangular_solve | solution.py:50
  1190.3 24.9 %custom-call.87 = f32[2,128,128]{2,1,0:T(8,128)} custom-call(f32[2,128,128]{2,1,0:T(8,128)} %copy.369), custom_call_target="Cholesky" | custom-call | tf_op jit(solution)/shard_map/jit(cholesky)/cholesky | solution.py:53
  1263.6 40.9 %custom-call.90 = f32[2,2,128,128]{2,3,1,0:T(8,128)} custom-call(f32[2,2,128,128]{3,2,1,0:T(8,128)} %pad_maximum_fusion.64), custom_call_target="InvertDiagBlocksLowerTriangular" | custom-call | tf_op jit(solution)/shard_map/jit(_cho_solve)/vmap()/triangular_solve | solution.py:55
  1332.0 31.7 %collective-permute-done.8 = f32[2,2,192,512]{3,2,1,0:T(8,128)S(1)} collective-permute-done((f32[2,2,192,512]{3,2,1,0:T(8,128)S(1)}, f32[2,2,192,512]{3,2,1,0:T(8,128)S(1)}, u32[]{:S(2)}, u32[]{:S(2)}) %collective-permute-start.8) | collective-permute-done | bytes 1572896 | tf_op jit(solution)/shard_map/ppermute | solution.py:27
  1389.3 25.3 %custom-call.91 = f32[2,128,128]{2,1,0:T(8,128)} custom-call(f32[2,128,128]{2,1,0:T(8,128)} %copy.385), custom_call_target="Cholesky" | custom-call | tf_op jit(solution)/shard_map/jit(cholesky)/cholesky | solution.py:49
  1462.9 40.9 %custom-call.94 = f32[2,2,128,128]{2,3,1,0:T(8,128)} custom-call(f32[2,2,128,128]{3,2,1,0:T(8,128)} %pad_maximum_fusion.65), custom_call_target="InvertDiagBlocksLowerTriangular" | custom-call | tf_op jit(solution)/shard_map/jit(_cho_solve)/vmap()/triangular_solve | solution.py:50
  1528.2 24.9 %custom-call.95 = f32[2,128,128]{2,1,0:T(8,128)} custom-call(f32[2,128,128]{2,1,0:T(8,128)} %copy.401), custom_call_target="Cholesky" | custom-call | tf_op jit(solution)/shard_map/jit(cholesky)/cholesky | solution.py:53
  1601.4 41.0 %custom-call.98 = f32[2,2,128,128]{2,3,1,0:T(8,128)} custom-call(f32[2,2,128,128]{3,2,1,0:T(8,128)} %pad_maximum_fusion.66), custom_call_target="InvertDiagBlocksLowerTriangular" | custom-call | tf_op jit(solution)/shard_map/jit(_cho_solve)/vmap()/triangular_solve | solution.py:55
  1668.6 30.4 %collective-permute-done.10 = f32[2,2,192,512]{3,2,1,0:T(8,128)S(1)} collective-permute-done((f32[2,2,192,512]{3,2,1,0:T(8,128)S(1)}, f32[2,2,192,512]{3,2,1,0:T(8,128)S(1)}, u32[]{:S(2)}, u32[]{:S(2)}) %collective-permute-start.10) | collective-permute-done | bytes 1572896 | tf_op jit(solution)/shard_map/ppermute | solution.py:27
  1710.5 23.6 %custom-call.99 = f32[2,128,128]{2,1,0:T(8,128)S(1)} custom-call(f32[2,128,128]{2,1,0:T(8,128)S(1)} %copy.417), custom_call_target="Cholesky" | custom-call | tf_op jit(solution)/shard_map/jit(cholesky)/cholesky | solution.py:49
  1779.2 40.9 %custom-call.102 = f32[2,2,128,128]{2,3,1,0:T(8,128)} custom-call(f32[2,2,128,128]{3,2,1,0:T(8,128)} %pad_maximum_fusion.67), custom_call_target="InvertDiagBlocksLowerTriangular" | custom-call | tf_op jit(solution)/shard_map/jit(_cho_solve)/vmap()/triangular_solve | solution.py:50
  1832.6 23.5 %custom-call.103 = f32[2,128,128]{2,1,0:T(8,128)S(1)} custom-call(f32[2,128,128]{2,1,0:T(8,128)S(1)} %cholesky.1108), custom_call_target="Cholesky" | custom-call | tf_op jit(solution)/shard_map/jit(cholesky)/cholesky | solution.py:53
  1890.3 39.6 %custom-call.106 = f32[2,2,128,128]{2,3,1,0:T(8,128)S(1)} custom-call(f32[2,2,128,128]{3,2,1,0:T(8,128)S(1)} %pad_maximum_fusion.68), custom_call_target="InvertDiagBlocksLowerTriangular" | custom-call | tf_op jit(solution)/shard_map/jit(_cho_solve)/vmap()/triangular_solve | solution.py:55
  (784 shorter events, 938.3 us)
Async XLA Ops:
  0.6 6.5 copy-start.125
  0.7 7.2 copy-start.126
  0.7 16.1 collective-permute-start
  2.5 14.2 collective-permute-start.1
  3.9 98.3 %copy-start.83 = (pred[64,64]{1,0:T(8,128)(4,1)}, pred[64,64]{1,0:T(8,128)(4,1)S(1)}, u32[]{:S(2)}) copy-start(pred[64,64]{1,0:T(8,128)(4,1)S(1)} %iota_compare_fusion.6) | copy-start | bytes 12292
  4.0 8.1 copy-start.66
  4.0 7.2 copy-start.124
  5.7 5.6 copy-start.129
  12.1 7.5 copy-start.51
  13.1 6.4 copy-start.67
  310.9 352.7 %copy-start.21 = (f32[2,2,192,192]{2,3,1,0:T(8,128)}, f32[2,2,192,192]{2,3,1,0:T(8,128)S(1)}, u32[]{:S(2)}) copy-start(f32[2,2,192,192]{2,3,1,0:T(8,128)S(1)} %fusion.1) | copy-start | bytes 1769476
  316.8 38.3 %copy-start.52 = (f32[2,1,2,192,192]{4,3,2,1,0:T(8,128)S(1)}, f32[2,1,2,192,192]{4,3,2,1,0:T(8,128)}, u32[]{:S(2)}) copy-start(f32[2,1,2,192,192]{4,3,2,1,0:T(8,128)} %copy-done.51) | copy-start | bytes 1769476
  316.8 38.3 %copy-start.54 = (f32[2,1,2,192,192]{4,3,2,1,0:T(8,128)S(1)}, f32[2,1,2,192,192]{4,3,2,1,0:T(8,128)}, u32[]{:S(2)}) copy-start(f32[2,1,2,192,192]{4,3,2,1,0:T(8,128)} %copy-done.53) | copy-start | bytes 1769476
  316.8 38.2 %collective-permute-start.2 = (f32[2,2,192,512]{3,2,1,0:T(8,128)}, f32[2,2,192,512]{3,2,1,0:T(8,128)S(1)}, u32[]{:S(2)}, u32[]{:S(2)}) collective-permute-start(f32[2,2,192,512]{3,2,1,0:T(8,128)} %copy.271), channel_id=1, source_target_pairs={{8,0},{16,8},{24,16},{32,24},{40,32},{48,40},{56,48},{64,56},{72,6... | collective-permute-start | bytes 4718600 | tf_op jit(solution)/shard_map/ppermute | solution.py:27
  365.4 24.9 %copy-start.98 = (f32[2,192,192]{1,2,0:T(8,128)}, f32[2,192,192]{1,2,0:T(8,128)S(1)}, u32[]{:S(2)}) copy-start(f32[2,192,192]{1,2,0:T(8,128)S(1)} %fusion.141) | copy-start | bytes 884740
  391.3 83.7 %copy-start.62 = (f32[2,192,192]{2,1,0:T(8,128)S(1)}, f32[2,192,192]{2,1,0:T(8,128)}, u32[]{:S(2)}) copy-start(f32[2,192,192]{2,1,0:T(8,128)} %get-tuple-element.159) | copy-start | bytes 884740
  475.0 11.6 copy-start.56
  492.0 61.2 %copy-start.84 = (pred[64,64]{1,0:T(8,128)(4,1)S(1)}, pred[64,64]{1,0:T(8,128)(4,1)}, u32[]{:S(2)}) copy-start(pred[64,64]{1,0:T(8,128)(4,1)} %copy-done.83) | copy-start | bytes 12292
  516.3 79.8 %copy-start.59 = (f32[128,192]{0,1:T(8,128)S(1)}, f32[128,192]{0,1:T(8,128)}, u32[]{:S(2)}) copy-start(f32[128,192]{0,1:T(8,128)} %slice.647) | copy-start | bytes 294916
  538.9 57.6 %copy-start.57 = (f32[64,192]{0,1:T(8,128)S(1)}, f32[64,192]{0,1:T(8,128)}, u32[]{:S(2)}) copy-start(f32[64,192]{0,1:T(8,128)} %slice.648) | copy-start | bytes 147460
  614.8 40.9 %collective-permute-start.4 = (f32[2,2,192,512]{3,2,1,0:T(8,128)S(1)}, f32[2,2,192,512]{3,2,1,0:T(8,128)S(1)}, u32[]{:S(2)}, u32[]{:S(2)}) collective-permute-start(f32[2,2,192,512]{3,2,1,0:T(8,128)S(1)} %pad_maximum_fusion.2), channel_id=1, source_target_pairs={{8,0},{16,8},{24,16},{32,24},{40,32},{48,40},{56,48},{64,56},{72,6... | collective-permute-start | bytes 4718600 | tf_op jit(solution)/shard_map/ppermute | solution.py:27
  621.2 41.3 %collective-permute-start.3 = (f32[2,2,192,512]{3,2,1,0:T(8,128)S(1)}, f32[2,2,192,512]{3,2,1,0:T(8,128)S(1)}, u32[]{:S(2)}, u32[]{:S(2)}) collective-permute-start(f32[2,2,192,512]{3,2,1,0:T(8,128)S(1)} %pad_maximum_fusion.2), channel_id=1, source_target_pairs={{0,8},{8,16},{16,24},{24,32},{32,40},{40,48},{48,56},{56,64},{64,7... | collective-permute-start | bytes 4718600 | tf_op jit(solution)/shard_map/ppermute | solution.py:27
  957.9 40.7 %collective-permute-start.6 = (f32[2,2,192,512]{3,2,1,0:T(8,128)S(1)}, f32[2,2,192,512]{3,2,1,0:T(8,128)S(1)}, u32[]{:S(2)}, u32[]{:S(2)}) collective-permute-start(f32[2,2,192,512]{3,2,1,0:T(8,128)S(1)} %pad_maximum_fusion.4), channel_id=1, source_target_pairs={{16,0},{24,8},{32,16},{40,24},{48,32},{56,40},{64,48},{72,56},{80,... | collective-permute-start | bytes 4718600 | tf_op jit(solution)/shard_map/ppermute | solution.py:27
  959.9 67.9 %collective-permute-start.5 = (f32[2,2,192,512]{3,2,1,0:T(8,128)S(1)}, f32[2,2,192,512]{3,2,1,0:T(8,128)S(1)}, u32[]{:S(2)}, u32[]{:S(2)}) collective-permute-start(f32[2,2,192,512]{3,2,1,0:T(8,128)S(1)} %pad_maximum_fusion.4), channel_id=1, source_target_pairs={{0,16},{8,24},{16,32},{24,40},{32,48},{40,56},{48,64},{56,72},{64,... | collective-permute-start | bytes 4718600 | tf_op jit(solution)/shard_map/ppermute | solution.py:27
  1322.8 40.9 %collective-permute-start.8 = (f32[2,2,192,512]{3,2,1,0:T(8,128)S(1)}, f32[2,2,192,512]{3,2,1,0:T(8,128)S(1)}, u32[]{:S(2)}, u32[]{:S(2)}) collective-permute-start(f32[2,2,192,512]{3,2,1,0:T(8,128)S(1)} %pad_maximum_fusion.6), channel_id=1, source_target_pairs={{32,0},{40,8},{48,16},{56,24},{64,32},{72,40},{80,48},{88,56},{96,... | collective-permute-start | bytes 4718600 | tf_op jit(solution)/shard_map/ppermute | solution.py:27
  1324.7 40.6 %collective-permute-start.7 = (f32[2,2,192,512]{3,2,1,0:T(8,128)S(1)}, f32[2,2,192,512]{3,2,1,0:T(8,128)S(1)}, u32[]{:S(2)}, u32[]{:S(2)}) collective-permute-start(f32[2,2,192,512]{3,2,1,0:T(8,128)S(1)} %pad_maximum_fusion.6), channel_id=1, source_target_pairs={{0,32},{8,40},{16,48},{24,56},{32,64},{40,72},{48,80},{56,88},{64,... | collective-permute-start | bytes 4718600 | tf_op jit(solution)/shard_map/ppermute | solution.py:27
  1660.7 38.4 %collective-permute-start.10 = (f32[2,2,192,512]{3,2,1,0:T(8,128)S(1)}, f32[2,2,192,512]{3,2,1,0:T(8,128)S(1)}, u32[]{:S(2)}, u32[]{:S(2)}) collective-permute-start(f32[2,2,192,512]{3,2,1,0:T(8,128)S(1)} %pad_maximum_fusion.8), channel_id=1, source_target_pairs={{64,0},{72,8},{80,16},{88,24},{96,32},{104,40},{112,48},{120,56},{... | collective-permute-start | bytes 4718600 | tf_op jit(solution)/shard_map/ppermute | solution.py:27
  1662.0 38.8 %collective-permute-start.9 = (f32[2,2,192,512]{3,2,1,0:T(8,128)S(1)}, f32[2,2,192,512]{3,2,1,0:T(8,128)S(1)}, u32[]{:S(2)}, u32[]{:S(2)}) collective-permute-start(f32[2,2,192,512]{3,2,1,0:T(8,128)S(1)} %pad_maximum_fusion.8), channel_id=1, source_target_pairs={{0,64},{8,72},{16,80},{24,88},{32,96},{40,104},{48,112},{56,120},{... | collective-permute-start | bytes 4718600 | tf_op jit(solution)/shard_map/ppermute | solution.py:27
  1831.7 58.1 %copy-start.85 = (pred[64,64]{1,0:T(8,128)(4,1)S(1)}, pred[64,64]{1,0:T(8,128)(4,1)}, u32[]{:S(2)}) copy-start(pred[64,64]{1,0:T(8,128)(4,1)} %copy-done.83) | copy-start | bytes 12292
  1856.1 73.8 %copy-start.60 = (f32[128,192]{0,1:T(8,128)S(1)}, f32[128,192]{0,1:T(8,128)}, u32[]{:S(2)}) copy-start(f32[128,192]{0,1:T(8,128)} %slice.647) | copy-start | bytes 294916
  1875.9 54.4 %copy-start.58 = (f32[64,192]{0,1:T(8,128)S(1)}, f32[64,192]{0,1:T(8,128)}, u32[]{:S(2)}) copy-start(f32[64,192]{0,1:T(8,128)} %slice.648) | copy-start | bytes 147460
  1938.3 12.8 collective-permute-start.11
  (111 other events, 201.3 us)
where the time goes:
time: 1970 us; the launch traced here: 1960 us
  other arithmetic  1300 us (66%)
  matrix products  237 us (12%)
  waiting for transfers between devices  201 us (10%)
  local copies, waits for them, and re-layouts  167 us (8%)
  starting transfers between devices  43.3 us (2%)
    another operation x50, other arithmetic, invert(): lower_imag = jnp.linalg.cholesky(imag)  374 us
    another operation x48, other arithmetic, invert(): lower_schur = jnp.linalg.cholesky(schur)  367 us
    another operation x27, other arithmetic, invert(): weighed = jax.scipy.linalg.cho_solve((lower_imag, True), real)  256 us
    another operation x24, other arithmetic, invert(): schur_inverse = jax.scipy.linalg.cho_solve((lower_schur, True), identity)  253 us
    ppermute x10, waiting for transfers between devices, shifted(): return lax.ppermute(array, axis, pairs)  201 us
    dot_general x94, matrix products, matmul_exact(): return jnp.matmul(left, right, precision=lax.Precision.HIGHEST)  102 us
    another operation x36, matrix products, invert(): weighed = jax.scipy.linalg.cho_solve((lower_imag, True), real)  48.4 us
    another operation x36, matrix products, invert(): schur_inverse = jax.scipy.linalg.cho_solve((lower_schur, True), identity)  43.8 us
  transfers between devices with their start and end apart: 12, of which 8 were waited for; matrix products, arithmetic and copies ran while one was open for 1% of the time, Pallas kernels for 0%

commit v1 on v0

--- a/solution.py
+++ b/solution.py
@@ -1,11 +1,119 @@
+import functools
+
 import jax
 import jax.numpy as jnp
 from jax import lax
+from jax.experimental import pallas as pl
+from jax.experimental.pallas import tpu as pltpu
 from jax.sharding import PartitionSpec as P
 
 broadening = 0.05
 energy_low = -1.2
 energy_step = 0.15
+
+
+N=192
+def split(x):
+    hi=x.astype(jnp.bfloat16); lo=(x-hi.astype(jnp.float32)).astype(jnp.bfloat16)
+    return hi,lo
+def tn(a,b):
+    return lax.dot_general(a,b,(((0,),(0,)),((),())),preferred_element_type=jnp.float32)
+def small_inverse8(mr,mi,b):
+    lane=lax.broadcasted_iota(jnp.int32,(b,128),1)
+    row8=lax.broadcasted_iota(jnp.int32,(8,128),0)
+    seg=(lane//b)*b
+    off8=(lane-seg)[0:8]
+    bc=lambda v: jnp.broadcast_to(v,(8,128))
+    for g in range(b//8):
+        o=8*g
+        Cr=[jnp.take_along_axis(mr,seg+(o+j),axis=1) for j in range(8)]
+        Ci=[jnp.take_along_axis(mi,seg+(o+j),axis=1) for j in range(8)]
+        cr=[x[o:o+8] for x in Cr]; ci=[x[o:o+8] for x in Ci]
+        for p in range(8):
+            dr=bc(cr[p][p:p+1]); di=bc(ci[p][p:p+1])
+            inv=1.0/(dr*dr+di*di)
+            er=dr*inv; ei=-di*inv
+            isrow=row8==p
+            pr,pi=cr[p],ci[p]
+            for j in range(8):
+                if j==p: continue
+                fr=bc(cr[j][p:p+1]); fi=bc(ci[j][p:p+1])
+                tr=fr*er-fi*ei; ti=fr*ei+fi*er
+                cr[j]=jnp.where(isrow,tr,cr[j]-(pr*tr-pi*ti))
+                ci[j]=jnp.where(isrow,ti,ci[j]-(pr*ti+pi*tr))
+            cr[p]=jnp.where(isrow,er,pi*ei-pr*er)
+            ci[p]=jnp.where(isrow,ei,-(pr*ei+pi*er))
+        ing=(off8>=o)&(off8<o+8)
+        G_r=jnp.where(ing,jnp.where(off8-o==row8,1.0,0.0),mr[o:o+8]); G_i=jnp.where(ing,0.0,mi[o:o+8])
+        Rr=None
+        for j in range(8):
+            gr=bc(G_r[j:j+1]); gi=bc(G_i[j:j+1])
+            a=cr[j]*gr-ci[j]*gi; c=cr[j]*gi+ci[j]*gr
+            Rr,Ri=(a,c) if Rr is None else (Rr+a,Ri+c)
+        out_r=[];out_i=[]
+        for h in range(b//8):
+            if h==g: out_r.append(Rr);out_i.append(Ri);continue
+            xr=jnp.where(ing,0.0,mr[8*h:8*h+8]); xi=jnp.where(ing,0.0,mi[8*h:8*h+8])
+            for j in range(8):
+                rr=bc(Rr[j:j+1]); ri=bc(Ri[j:j+1])
+                ar_=Cr[j][8*h:8*h+8]; ai_=Ci[j][8*h:8*h+8]
+                xr=xr-(ar_*rr-ai_*ri); xi=xi-(ar_*ri+ai_*rr)
+            out_r.append(xr);out_i.append(xi)
+        mr=jnp.concatenate(out_r,0); mi=jnp.concatenate(out_i,0)
+    return mr,mi
+def inverse_body(B,b,pr,pi,xr,xi,ar,ai):
+    W=256
+    for e in range(B):
+        ar[e,:,0:N]=pr[e]; ai[e,:,0:N]=pi[e]
+        ar[e,:,N:]=jnp.zeros((N,W-N),jnp.float32); ai[e,:,N:]=jnp.zeros((N,W-N),jnp.float32)
+    lane=lax.broadcasted_iota(jnp.int32,(b,W),1)
+    row=lax.broadcasted_iota(jnp.int32,(b,W),0)
+    def step(k,_):
+        o=pl.multiple_of(k*b,b)
+        rows=[(ar[e,pl.ds(o,b),:],ai[e,pl.ds(o,b),:]) for e in range(B)]
+        mr=jnp.zeros((b,128),jnp.float32); mi=mr
+        l128=lax.broadcasted_iota(jnp.int32,(b,128),1)
+        for e in range(B):
+            sh=lax.rem(W-o+e*b,W)
+            qr=pltpu.roll(rows[e][0],sh,1)[:,0:128]; qi=pltpu.roll(rows[e][1],sh,1)[:,0:128]
+            s=(l128>=e*b)&(l128<(e+1)*b)
+            mr=jnp.where(s,qr,mr); mi=jnp.where(s,qi,mi)
+        if B*b<128:
+            l=l128-b*(l128//b)
+            r_=lax.broadcasted_iota(jnp.int32,(b,128),0)
+            mr=jnp.where((l128>=B*b)&(l==r_),1.0,mr)
+        mr,mi=small_inverse8(mr,mi,b)
+        for e in range(B):
+            rr,ri=rows[e]
+            dr=mr[:,e*b:(e+1)*b]; di=mi[:,e*b:(e+1)*b]
+            inblk=(lane>=o)&(lane<o+b)
+            eye=lane-o==row
+            r2=jnp.where(inblk,jnp.where(eye,-1.0,0.0),rr); i2=jnp.where(inblk,0.0,ri)
+            drh,drl=split(dr); dih,dil=split(di)
+            r2h,r2l=split(r2); i2h,i2l=split(i2)
+            lhs=jnp.concatenate([drh,dih,drl,dil,drh,dih],0)
+            Rr=tn(lhs,jnp.concatenate([r2h,-i2h,r2h,-i2h,r2l,-i2l],0))
+            Ri=tn(lhs,jnp.concatenate([i2h,r2h,i2h,r2h,i2l,r2l],0))
+            Rrh,Rrl=split(Rr); Rih,Ril=split(Ri)
+            rh,rl=split(rr); ih,il=split(ri)
+            lhs=jnp.concatenate([rh,ih,rl,il,rh,ih],0)[:,0:N]
+            Ur=tn(lhs,jnp.concatenate([Rrh,-Rih,Rrh,-Rih,Rrl,-Ril],0))
+            Ui=tn(lhs,jnp.concatenate([Rih,Rrh,Rih,Rrh,Ril,Rrl],0))
+            lN=lax.broadcasted_iota(jnp.int32,(N,W),1)
+            m=(lN>=o)&(lN<o+b)
+            ar[e]=jnp.where(m,0.0,ar[e])-Ur
+            ai[e]=jnp.where(m,0.0,ai[e])-Ui
+            ar[e,pl.ds(o,b),:]=Rr; ai[e,pl.ds(o,b),:]=Ri
+        return 0
+    lax.fori_loop(0,N//b,step,0)
+    for e in range(B):
+        xr[e]=-ar[e,:,0:N]; xi[e]=-ai[e,:,0:N]
+def inverse(pr,pi,b=64):
+    B=pr.shape[0]
+    f=jax.ShapeDtypeStruct((B,N,N),jnp.float32)
+    return pl.pallas_call(functools.partial(inverse_body,B,b),out_shape=(f,f),
+      in_specs=[pl.BlockSpec(memory_space=pltpu.VMEM)]*2,out_specs=[pl.BlockSpec(memory_space=pltpu.VMEM)]*2,
+      scratch_shapes=[pltpu.VMEM((B,N,256),jnp.float32)]*2,name="block_inverse")(pr,pi)
 
 
 def padded(block, sides, width):
@@ -46,14 +154,7 @@
     imag = block[..., 1, :, :, :]
     real = 0.5 * (real + jnp.swapaxes(real, -1, -2))
     imag = 0.5 * (imag + jnp.swapaxes(imag, -1, -2))
-    lower_imag = jnp.linalg.cholesky(imag)
-    weighed = jax.scipy.linalg.cho_solve((lower_imag, True), real)
-    schur = imag + matmul_exact(real, weighed)
-    schur = 0.5 * (schur + jnp.swapaxes(schur, -1, -2))
-    lower_schur = jnp.linalg.cholesky(schur)
-    identity = jnp.broadcast_to(jnp.eye(schur.shape[-1], dtype=schur.dtype), schur.shape)
-    schur_inverse = jax.scipy.linalg.cho_solve((lower_schur, True), identity)
-    return jnp.stack([matmul_exact(weighed, schur_inverse), -schur_inverse], axis=-4)
+    return jnp.stack(inverse(real, imag), axis=-4)
 
 
 def per_device(

time: 1970 us -> 589 us (0.30)
  other arithmetic: 1300 us -> 49.9 us
  matrix products: 237 us -> 125 us
  Pallas kernels: 0 us -> 78.6 us
  local copies, waits for them, and re-layouts: 167 us -> 96.1 us
    another operation x149 -> x0, other arithmetic: 1250 us -> none  [the longest x50 374 us: invert(): lower_imag = jnp.linalg.cholesky(imag)]
    another operation x96 -> x0, matrix products: 132 us -> none  [the longest x36 48.4 us: invert(): weighed = jax.scipy.linalg.cho_solve((lower_imag, True), real)]
    pallas_call x0 -> x6, Pallas kernels: none -> 78.6 us  [inverse(): pl.pallas_call(functools.partial(inverse_body, B, b), out_shape=(f, f), i...]
    another operation x85 -> x0, local copies, waits for them, and re-layouts: 69.1 us -> none  [the longest x24 27.4 us: invert(): lower_imag = jnp.linalg.cholesky(imag)]
    unnamed x261 -> x153, local copies, waits for them, and re-layouts: 37.4 us -> 9.94 us
    dot_general x94 -> x82, matrix products: 102 us -> 122 us  [matmul_exact(): return jnp.matmul(left, right, precision=lax.Precision.HIGHEST)]
  transfers between devices with their start and end apart: 12 -> 12, of which waited for: 8 -> 7; matrix products, arithmetic and copies ran while one was open for 1% -> 12% of each run, Pallas kernels for 0% -> 0%
where the time goes in v1:
time: 589 us; the launch traced here: 579 us
  waiting for transfers between devices  182 us (31%)
  matrix products  125 us (21%)
  local copies, waits for them, and re-layouts  96.1 us (16%)
  Pallas kernels  78.6 us (13%)
  other arithmetic  49.9 us (8%)
  starting transfers between devices  44.3 us (8%)
    ppermute x10, waiting for transfers between devices, shifted(): return lax.ppermute(array, axis, pairs)  182 us
    dot_general x82, matrix products, matmul_exact(): return jnp.matmul(left, right, precision=lax.Precision.HIGHEST)  122 us
    pallas_call x6, Pallas kernels, inverse(): pl.pallas_call(functools.partial(inverse_body, B, b), out_shape=(f, f), i...  78.6 us
    ppermute x10, starting transfers between devices, shifted(): return lax.ppermute(array, axis, pairs)  41.2 us
    sub x8, local copies, waits for them, and re-layouts, complex_product(): matmul_exact(left[..., 0, :, :, :], right[..., 0, :, :, :])  18.7 us
    add x8, local copies, waits for them, and re-layouts, complex_product(): matmul_exact(left[..., 0, :, :, :], right[..., 1, :, :, :])  17.7 us
    squeeze x12, local copies, waits for them, and re-layouts, invert(): imag = block[..., 1, :, :, :]  14.1 us
    mul x6, other arithmetic, invert(): imag = 0.5 * (imag + jnp.swapaxes(imag, -1, -2))  12.2 us
  transfers between devices with their start and end apart: 12, of which 7 were waited for; matrix products, arithmetic and copies ran while one was open for 12% of the time, Pallas kernels for 0%

profile of v1, /device:TPU:32, one launch (start us, length us, event | category | flops | bytes accessed | tf_op | source)
XLA Modules:
  0.0 578.8 jit_solution(3603760764803555934)
XLA Ops:
  30.5 13.1 %block_inverse.7 = (f32[2,192,192]{2,1,0:T(8,128)}, f32[2,192,192]{2,1,0:T(8,128)}) custom-call(f32[2,192,192]{2,1,0:T(8,128)} %copy.248.pr, f32[2,192,192]{2,1,0:T(8,128)} %copy.249.pi), custom_call_target="tpu_custom_call" | custom-call | tf_op jit(solution)/shard_map/while/body/eval_jaxpr/block_inverse/pallas_call | solution.py:114
  56.6 4.7 collective-permute-start.2
  66.2 28.5 %collective-permute-done.2 = f32[2,2,192,512]{3,2,1,0:T(8,128)} collective-permute-done((f32[2,2,192,512]{3,2,1,0:T(8,128)}, f32[2,2,192,512]{3,2,1,0:T(8,128)}, u32[]{:S(2)}, u32[]{:S(2)}) %collective-permute-start.2) | collective-permute-done | bytes 1572896 | tf_op jit(solution)/shard_map/ppermute | solution.py:135
  115.1 12.9 %block_inverse.8 = (f32[2,192,192]{2,1,0:T(8,128)}, f32[2,192,192]{2,1,0:T(8,128)}) custom-call(f32[2,192,192]{2,1,0:T(8,128)} %copy.259.pr, f32[2,192,192]{2,1,0:T(8,128)} %copy.260.pi), custom_call_target="tpu_custom_call" | custom-call | tf_op jit(solution)/shard_map/block_inverse/pallas_call | solution.py:114
  133.7 6.9 %collective-permute-start.4 = (f32[2,2,192,512]{3,2,1,0:T(8,128)}, f32[2,2,192,512]{3,2,1,0:T(8,128)S(1)}, u32[]{:S(2)}, u32[]{:S(2)}) collective-permute-start(f32[2,2,192,512]{3,2,1,0:T(8,128)} %pad_maximum_fusion.5), channel_id=1, source_target_pairs={{8,0},{16,8},{24,16},{32,24},{40,32},{48,40},{56,48},{64,56},{72,6... | collective-permute-start | bytes 4718600 | tf_op jit(solution)/shard_map/ppermute | solution.py:135
  142.5 32.4 %collective-permute-done.4 = f32[2,2,192,512]{3,2,1,0:T(8,128)S(1)} collective-permute-done((f32[2,2,192,512]{3,2,1,0:T(8,128)}, f32[2,2,192,512]{3,2,1,0:T(8,128)S(1)}, u32[]{:S(2)}, u32[]{:S(2)}) %collective-permute-start.4) | collective-permute-done | bytes 1572896 | tf_op jit(solution)/shard_map/ppermute | solution.py:135
  186.6 2.8 convolution_add_fusion.10
  214.0 13.1 %block_inverse.9 = (f32[2,192,192]{2,1,0:T(8,128)}, f32[2,192,192]{2,1,0:T(8,128)}) custom-call(f32[2,192,192]{2,1,0:T(8,128)} %copy.275.pr, f32[2,192,192]{2,1,0:T(8,128)} %copy.276.pi), custom_call_target="tpu_custom_call" | custom-call | tf_op jit(solution)/shard_map/block_inverse/pallas_call | solution.py:114
  234.9 3.4 collective-permute-start.6
  238.4 4.1 collective-permute-start.5
  242.5 33.3 %collective-permute-done.6 = f32[2,2,192,512]{3,2,1,0:T(8,128)S(1)} collective-permute-done((f32[2,2,192,512]{3,2,1,0:T(8,128)}, f32[2,2,192,512]{3,2,1,0:T(8,128)S(1)}, u32[]{:S(2)}, u32[]{:S(2)}) %collective-permute-start.6) | collective-permute-done | bytes 1572896 | tf_op jit(solution)/shard_map/ppermute | solution.py:135
  283.7 3.1 convolution_subtract_fusion.6
  289.2 18.3 %collective-permute-done.5 = f32[2,2,192,512]{3,2,1,0:T(8,128)} collective-permute-done((f32[2,2,192,512]{3,2,1,0:T(8,128)}, f32[2,2,192,512]{3,2,1,0:T(8,128)}, u32[]{:S(2)}, u32[]{:S(2)}) %collective-permute-start.5) | collective-permute-done | bytes 1572896 | tf_op jit(solution)/shard_map/ppermute | solution.py:135
  309.8 3.1 convolution_add_fusion.7
  317.8 3.1 convolution_subtract_fusion.7
  339.8 13.2 %block_inverse.10 = (f32[2,192,192]{2,1,0:T(8,128)}, f32[2,192,192]{2,1,0:T(8,128)}) custom-call(f32[2,192,192]{2,1,0:T(8,128)} %copy.297.pr, f32[2,192,192]{2,1,0:T(8,128)} %copy.298.pi), custom_call_target="tpu_custom_call" | custom-call | tf_op jit(solution)/shard_map/block_inverse/pallas_call | solution.py:114
  362.8 5.4 collective-permute-start.7
  368.2 31.9 %collective-permute-done.8 = f32[2,2,192,512]{3,2,1,0:T(8,128)S(1)} collective-permute-done((f32[2,2,192,512]{3,2,1,0:T(8,128)}, f32[2,2,192,512]{3,2,1,0:T(8,128)S(1)}, u32[]{:S(2)}, u32[]{:S(2)}) %collective-permute-start.8) | collective-permute-done | bytes 1572896 | tf_op jit(solution)/shard_map/ppermute | solution.py:135
  408.1 3.1 convolution_subtract_fusion.3
  416.0 3.1 convolution_add_fusion.4
  423.9 3.1 convolution_subtract_fusion.4
  429.5 2.9 fusion.86
  446.3 13.1 %block_inverse.11 = (f32[2,192,192]{2,1,0:T(8,128)}, f32[2,192,192]{2,1,0:T(8,128)}) custom-call(f32[2,192,192]{2,1,0:T(8,128)} %copy.319.pr, f32[2,192,192]{2,1,0:T(8,128)} %copy.320.pi), custom_call_target="tpu_custom_call" | custom-call | tf_op jit(solution)/shard_map/block_inverse/pallas_call | solution.py:114
  468.5 7.5 %collective-permute-start.9 = (f32[2,2,192,512]{3,2,1,0:T(8,128)}, f32[2,2,192,512]{3,2,1,0:T(8,128)}, u32[]{:S(2)}, u32[]{:S(2)}) collective-permute-start(f32[2,2,192,512]{3,2,1,0:T(8,128)} %pad_maximum_fusion.8), channel_id=1, source_target_pairs={{0,64},{8,72},{16,80},{24,88},{32,96},{40,104},{48,112},{56,120},{... | collective-permute-start | bytes 4718600 | tf_op jit(solution)/shard_map/ppermute | solution.py:135
  476.0 30.2 %collective-permute-done.10 = f32[2,2,192,512]{3,2,1,0:T(8,128)S(1)} collective-permute-done((f32[2,2,192,512]{3,2,1,0:T(8,128)}, f32[2,2,192,512]{3,2,1,0:T(8,128)S(1)}, u32[]{:S(2)}, u32[]{:S(2)}) %collective-permute-start.10) | collective-permute-done | bytes 1572896 | tf_op jit(solution)/shard_map/ppermute | solution.py:135
  514.2 3.1 convolution_subtract_fusion
  522.1 3.1 convolution_add_fusion.1
  530.1 3.1 convolution_subtract_fusion.1
  535.6 3.3 fusion.84
  541.8 13.2 %block_inverse.12 = (f32[2,192,192]{2,1,0:T(8,128)}, f32[2,192,192]{2,1,0:T(8,128)}) custom-call(f32[2,192,192]{2,1,0:T(8,128)} %fusion.99.pr, f32[2,192,192]{2,1,0:T(8,128)} %broadcast_multiply_fusion.1.pi), custom_call_target="tpu_custom_call" | custom-call | tf_op jit(solution)/shard_map/block_inverse/pallas_call | solution.py:114
  560.6 4.1 collective-permute-start.11
  566.3 7.5 %collective-permute-done.11 = f32[2,2,192,128]{3,2,1,0:T(8,128)S(1)} collective-permute-done((f32[2,2,192,128]{3,2,1,0:T(8,128)S(1)}, f32[2,2,192,128]{3,2,1,0:T(8,128)S(1)}, u32[]{:S(2)}, u32[]{:S(2)}) %collective-permute-start.11) | collective-permute-done | bytes 393248 | tf_op jit(solution)/shard_map/ppermute | solution.py:135
  (329 shorter events, 242.5 us)
Async XLA Ops:
  0.6 6.4 %copy-start.65 = (f32[4]{0:T(128)S(1)}, f32[4]{0:T(128)}, u32[]{:S(2)}) copy-start(f32[4]{0:T(128)} %param.14) | copy-start | bytes 52
  0.7 7.1 %copy-start.66 = (s32[4]{0:T(128)S(1)}, s32[4]{0:T(128)}, u32[]{:S(2)}) copy-start(s32[4]{0:T(128)} %param.15) | copy-start | bytes 52
  0.7 14.8 %collective-permute-start = (f32[2,2,192]{2,1,0:T(2,128)}, f32[2,2,192]{2,1,0:T(2,128)S(1)}, u32[]{:S(2)}, u32[]{:S(2)}) collective-permute-start(f32[2,2,192]{2,1,0:T(2,128)} %param.13), channel_id=1, source_target_pairs={{0,1},{1,2},{2,3},{3,4},{4,5},{5,6},{6,7},{8,9},{9,10},{10,11},{11... | collective-permute-start | bytes 9224 | tf_op jit(solution)/shard_map/ppermute | solution.py:124
  2.5 12.9 %collective-permute-start.1 = (f32[2,2,192]{2,1,0:T(2,128)}, f32[2,2,192]{2,1,0:T(2,128)S(1)}, u32[]{:S(2)}, u32[]{:S(2)}) collective-permute-start(f32[2,2,192]{2,1,0:T(2,128)} %param.13), channel_id=1, source_target_pairs={{1,0},{2,1},{3,2},{4,3},{5,4},{6,5},{7,6},{9,8},{10,9},{11,10},{12... | collective-permute-start | bytes 9224 | tf_op jit(solution)/shard_map/ppermute | solution.py:127
  3.9 7.7 %copy-start.64 = (f32[192,192]{1,0:T(8,128)S(1)}, f32[192,192]{1,0:T(8,128)}, u32[]{:S(2)}) copy-start(f32[192,192]{1,0:T(8,128)} %param.9) | copy-start | bytes 442372
  3.9 7.8 %copy-start.63 = (f32[2,2,2,192,128]{4,3,2,1,0:T(8,128)S(1)}, f32[2,2,2,192,128]{4,3,2,1,0:T(8,128)}, u32[]{:S(2)}) copy-start(f32[2,2,2,192,128]{4,3,2,1,0:T(8,128)} %param.8) | copy-start | bytes 2359300
  7.0 5.6 copy-start.67
  7.0 5.5 copy-start.69
  13.1 5.3 copy-start.39
  13.1 5.2 copy-start.52
  51.9 11.5 %copy-start.2 = (f32[1,2,2,192,512]{4,3,2,1,0:T(8,128)}, f32[1,2,2,192,512]{4,3,2,1,0:T(8,128)S(1)}, u32[]{:S(2)}) copy-start(f32[1,2,2,192,512]{4,3,2,1,0:T(8,128)S(1)} %maximum_add_fusion) | copy-start | bytes 4718596
  54.2 132.4 %copy-start.8 = (f32[2,2,192,192]{3,2,1,0:T(8,128)}, f32[2,2,192,192]{3,2,1,0:T(8,128)S(1)}, u32[]{:S(2)}) copy-start(f32[2,2,192,192]{3,2,1,0:T(8,128)S(1)} %fusion.1) | copy-start | bytes 1769476
  55.0 6.3 %copy-start.53 = (f32[1,2,2,192,128]{4,3,2,1,0:T(8,128)S(1)}, f32[1,2,2,192,128]{4,3,2,1,0:T(8,128)}, u32[]{:S(2)}) copy-start(f32[1,2,2,192,128]{4,3,2,1,0:T(8,128)} %get-tuple-element.96) | copy-start | bytes 1179652
  56.6 38.1 %collective-permute-start.2 = (f32[2,2,192,512]{3,2,1,0:T(8,128)}, f32[2,2,192,512]{3,2,1,0:T(8,128)}, u32[]{:S(2)}, u32[]{:S(2)}) collective-permute-start(f32[2,2,192,512]{3,2,1,0:T(8,128)} %pad_maximum_fusion.3), channel_id=1, source_target_pairs={{8,0},{16,8},{24,16},{32,24},{40,32},{48,40},{56,48},{64,56},{72,6... | collective-permute-start | bytes 4718600 | tf_op jit(solution)/shard_map/ppermute | solution.py:135
  105.1 4.2 copy-start.15
  133.7 41.3 %collective-permute-start.4 = (f32[2,2,192,512]{3,2,1,0:T(8,128)}, f32[2,2,192,512]{3,2,1,0:T(8,128)S(1)}, u32[]{:S(2)}, u32[]{:S(2)}) collective-permute-start(f32[2,2,192,512]{3,2,1,0:T(8,128)} %pad_maximum_fusion.5), channel_id=1, source_target_pairs={{8,0},{16,8},{24,16},{32,24},{40,32},{48,40},{56,48},{64,56},{72,6... | collective-permute-start | bytes 4718600 | tf_op jit(solution)/shard_map/ppermute | solution.py:135
  140.6 44.0 %collective-permute-start.3 = (f32[2,2,192,512]{3,2,1,0:T(8,128)}, f32[2,2,192,512]{3,2,1,0:T(8,128)}, u32[]{:S(2)}, u32[]{:S(2)}) collective-permute-start(f32[2,2,192,512]{3,2,1,0:T(8,128)} %pad_maximum_fusion.5), channel_id=1, source_target_pairs={{0,8},{8,16},{16,24},{24,32},{32,40},{40,48},{48,56},{56,64},{64,7... | collective-permute-start | bytes 4718600 | tf_op jit(solution)/shard_map/ppermute | solution.py:135
  233.6 42.2 %copy-start.29 = (f32[2,2,192,192]{2,3,1,0:T(8,128)S(1)}, f32[2,2,192,192]{2,3,1,0:T(8,128)}, u32[]{:S(2)}) copy-start(f32[2,2,192,192]{2,3,1,0:T(8,128)} %get-tuple-element.79) | copy-start | bytes 1769476
  234.9 40.9 %collective-permute-start.6 = (f32[2,2,192,512]{3,2,1,0:T(8,128)}, f32[2,2,192,512]{3,2,1,0:T(8,128)S(1)}, u32[]{:S(2)}, u32[]{:S(2)}) collective-permute-start(f32[2,2,192,512]{3,2,1,0:T(8,128)} %pad_maximum_fusion.6), channel_id=1, source_target_pairs={{16,0},{24,8},{32,16},{40,24},{48,32},{56,40},{64,48},{72,56},{80,... | collective-permute-start | bytes 4718600 | tf_op jit(solution)/shard_map/ppermute | solution.py:135
  238.4 69.1 %collective-permute-start.5 = (f32[2,2,192,512]{3,2,1,0:T(8,128)}, f32[2,2,192,512]{3,2,1,0:T(8,128)}, u32[]{:S(2)}, u32[]{:S(2)}) collective-permute-start(f32[2,2,192,512]{3,2,1,0:T(8,128)} %pad_maximum_fusion.6), channel_id=1, source_target_pairs={{0,16},{8,24},{16,32},{24,40},{32,48},{40,56},{48,64},{56,72},{64,... | collective-permute-start | bytes 4718600 | tf_op jit(solution)/shard_map/ppermute | solution.py:135
  289.2 20.6 %copy-start.23 = (f32[2,2,192,192]{2,3,1,0:T(8,128)S(1)}, f32[2,2,192,192]{2,3,1,0:T(8,128)}, u32[]{:S(2)}) copy-start(f32[2,2,192,192]{2,3,1,0:T(8,128)} %get-tuple-element.77) | copy-start | bytes 1769476
  359.6 40.5 %copy-start.31 = (f32[2,2,192,192]{2,3,1,0:T(8,128)S(1)}, f32[2,2,192,192]{2,3,1,0:T(8,128)}, u32[]{:S(2)}) copy-start(f32[2,2,192,192]{2,3,1,0:T(8,128)} %get-tuple-element.76) | copy-start | bytes 1769476
  360.9 39.2 %collective-permute-start.8 = (f32[2,2,192,512]{3,2,1,0:T(8,128)}, f32[2,2,192,512]{3,2,1,0:T(8,128)S(1)}, u32[]{:S(2)}, u32[]{:S(2)}) collective-permute-start(f32[2,2,192,512]{3,2,1,0:T(8,128)} %pad_maximum_fusion.7), channel_id=1, source_target_pairs={{32,0},{40,8},{48,16},{56,24},{64,32},{72,40},{80,48},{88,56},{96,... | collective-permute-start | bytes 4718600 | tf_op jit(solution)/shard_map/ppermute | solution.py:135
  362.8 50.8 %collective-permute-start.7 = (f32[2,2,192,512]{3,2,1,0:T(8,128)}, f32[2,2,192,512]{3,2,1,0:T(8,128)}, u32[]{:S(2)}, u32[]{:S(2)}) collective-permute-start(f32[2,2,192,512]{3,2,1,0:T(8,128)} %pad_maximum_fusion.7), channel_id=1, source_target_pairs={{0,32},{8,40},{16,48},{24,56},{32,64},{40,72},{48,80},{56,88},{64,... | collective-permute-start | bytes 4718600 | tf_op jit(solution)/shard_map/ppermute | solution.py:135
  429.5 3.4 copy-start.20
  465.9 40.3 %copy-start.33 = (f32[2,2,192,192]{2,3,1,0:T(8,128)S(1)}, f32[2,2,192,192]{2,3,1,0:T(8,128)}, u32[]{:S(2)}) copy-start(f32[2,2,192,192]{2,3,1,0:T(8,128)} %get-tuple-element.73) | copy-start | bytes 1769476
  467.2 39.0 %collective-permute-start.10 = (f32[2,2,192,512]{3,2,1,0:T(8,128)}, f32[2,2,192,512]{3,2,1,0:T(8,128)S(1)}, u32[]{:S(2)}, u32[]{:S(2)}) collective-permute-start(f32[2,2,192,512]{3,2,1,0:T(8,128)} %pad_maximum_fusion.8), channel_id=1, source_target_pairs={{64,0},{72,8},{80,16},{88,24},{96,32},{104,40},{112,48},{120,56},{... | collective-permute-start | bytes 4718600 | tf_op jit(solution)/shard_map/ppermute | solution.py:135
  468.5 51.2 %collective-permute-start.9 = (f32[2,2,192,512]{3,2,1,0:T(8,128)}, f32[2,2,192,512]{3,2,1,0:T(8,128)}, u32[]{:S(2)}, u32[]{:S(2)}) collective-permute-start(f32[2,2,192,512]{3,2,1,0:T(8,128)} %pad_maximum_fusion.8), channel_id=1, source_target_pairs={{0,64},{8,72},{16,80},{24,88},{32,96},{40,104},{48,112},{56,120},{... | collective-permute-start | bytes 4718600 | tf_op jit(solution)/shard_map/ppermute | solution.py:135
  535.6 3.4 copy-start.37
  535.6 3.8 copy-start.38
  540.8 14.2 %copy-start.51 = (f32[2,2,192,128]{2,3,1,0:T(8,128)S(1)}, f32[2,2,192,128]{2,3,1,0:T(8,128)}, u32[]{:S(2)}) copy-start(f32[2,2,192,128]{2,3,1,0:T(8,128)} %fusion.84) | copy-start | bytes 1179652
  560.6 13.3 %collective-permute-start.11 = (f32[2,2,192,128]{3,2,1,0:T(8,128)S(1)}, f32[2,2,192,128]{3,2,1,0:T(8,128)S(1)}, u32[]{:S(2)}, u32[]{:S(2)}) collective-permute-start(f32[2,2,192,128]{3,2,1,0:T(8,128)S(1)} %get-tuple-element.106), channel_id=1, source_target_pairs={{0,8},{8,16},{16,24},{24,32},{32,40},{40,48},{48,56},{56,64},{64,7... | collective-permute-start | bytes 1179656 | tf_op jit(solution)/shard_map/ppermute | solution.py:135
  (54 other events, 116.3 us)
